TPU v7x, 32 devices: a whole 2x2x4 slice. The times are simulated.
32 devices in a mesh: replica: 8 (over z, core), group: 4 (over y, x).
Axes of the slice: x: 2, y: 2, z: 4, core: 2. Of those that a mesh axis runs over, the one named last changes fastest.
Arguments:
- tokens: bfloat16 [4096, 2048], P(('replica', 'group')), may hold values from -6 to 6
- lengths: int32 [8], P('replica'), may hold values from 128 to 512, as said below
- exit_layers: int32 [4096], P(('replica', 'group')), may hold values from 7 to 20, as said below
- pre_gain: bfloat16 [2048], P('group'), may hold values from 0.099609375 to 1.8984375
- pre_shift: bfloat16 [2048], P('group'), may hold values from -3 to 3
- query_weight: bfloat16 [2048, 2048], P('group'), may hold values from -0.1875 to 0.1875
- query_bias: bfloat16 [2048], P('group'), may hold values from -3 to 3
- key_weight: bfloat16 [2048, 2048], P('group'), may hold values from -0.1875 to 0.1875
- value_weight: bfloat16 [2048, 2048], P('group'), may hold values from -0.125 to 0.125
- value_bias: bfloat16 [2048], P('group'), may hold values from -3 to 3
- out_weight: bfloat16 [2048, 2048], P('group'), may hold values from -0.5 to 0.5
- out_bias: bfloat16 [2048], P('group'), may hold values from -1.75 to 1.75
- mid_gain: bfloat16 [2048], P('group'), may hold values from 0.099609375 to 1.8984375
- mid_shift: bfloat16 [2048], P('group'), may hold values from -3 to 3
- up_weight: bfloat16 [2048, 8192], P(None, 'group'), may hold values from -0.125 to 0.125
- up_bias: bfloat16 [8192], P('group'), may hold values from -3 to 3
- down_weight: bfloat16 [8192, 2048], P('group'), may hold values from -0.0625 to 0.0625
- down_bias: bfloat16 [2048], P('group'), may hold values from -1.75 to 1.75
- cotangent: bfloat16 [4096, 2048], P(('replica', 'group')), may hold values from -6 to 6
Outputs:
- output: bfloat16 [4096, 2048], P(('replica', 'group'))
- token_grad: bfloat16 [4096, 2048], P(('replica', 'group'))
- pre_gain_grad: float32 [2048], P('group')
- pre_shift_grad: float32 [2048], P('group')
- query_weight_grad: float32 [2048, 2048], P('group')
- query_bias_grad: float32 [2048], P('group')
- key_weight_grad: float32 [2048, 2048], P('group')
- value_weight_grad: float32 [2048, 2048], P('group')
- value_bias_grad: float32 [2048], P('group')
- out_weight_grad: float32 [2048, 2048], P('group')
- out_bias_grad: float32 [2048], P('group')
- mid_gain_grad: float32 [2048], P('group')
- mid_shift_grad: float32 [2048], P('group')
- up_weight_grad: float32 [2048, 8192], P(None, 'group')
- up_bias_grad: float32 [8192], P('group')
- down_weight_grad: float32 [8192, 2048], P('group')
- down_bias_grad: float32 [2048], P('group')
Inputs may be any that keep to these rules, and one draw needn't show every extreme that they name: `lengths`: some sequence has length 512 and some other has length 128. Within each sequence, exit_layers never rise from one position to the next.
All inputs are finite; a program needn't handle non-finite values.
Results may differ from a plain program's by a relative error of at most 0.02.
Values may be sent and summed in bfloat16 or wider, within the bound.
No kernel may reach another device: no remote copies, remote signals or barrier semaphores. Data moves between devices by JAX's collectives and lax.ppermute only.
A program may use at most 640 MiB of HBM per device.

v0:
```python
import jax
import jax.numpy as jnp
from jax import lax
from jax.sharding import PartitionSpec as P

D = 2048
H = 32
HD = 64
LAYER = 12


def layer_norm(values):
    center = values - jnp.mean(values, -1, keepdims=True)
    spread = jnp.mean(center * center, -1, keepdims=True)
    factor = lax.rsqrt(spread + 1e-05)
    return (center * factor, factor)


def norm_back(grad, normal, factor):
    return factor * (
        grad
        - jnp.mean(grad, -1, keepdims=True)
        - normal * jnp.mean(grad * normal, -1, keepdims=True)
    )


def gelu(values):
    return (
        0.5
        * values
        * (1.0 + jnp.tanh(0.7978845608 * (values + 0.044715 * values * values * values)))
    )


def gelu_back(values, grad):
    inner = 0.7978845608 * (values + 0.044715 * values * values * values)
    tangent = jnp.tanh(inner)
    slope = 0.5 * (1.0 + tangent) + 0.5 * values * (1.0 - tangent * tangent) * 0.7978845608 * (
        1.0 + 3.0 * 0.044715 * values * values
    )
    return grad * slope


def split_heads(matrix):
    groups = max(1, H // 8)
    return matrix.reshape(matrix.shape[0], groups, H // groups, HD).transpose(1, 0, 2, 3)


def join_heads(heads):
    return heads.transpose(1, 0, 2, 3).reshape(heads.shape[1], D)


def score_block(query_group, key_group, allowed):
    scores = (
        jnp.einsum("qhd,khd->hqk", query_group, key_group, preferred_element_type=jnp.float32)
        * 0.125
    )
    return jnp.where(allowed[None], scores, -1e30)


def matmul(left, right):
    return jnp.dot(left, right, preferred_element_type=jnp.float32)


def column_sums(matrix):
    return jnp.sum(matrix.astype(jnp.float32), 0)


def shards(
    tokens,
    lengths,
    exit_layers,
    pre_gain,
    pre_shift,
    query_weight,
    query_bias,
    key_weight,
    value_weight,
    value_bias,
    out_weight,
    out_bias,
    mid_gain,
    mid_shift,
    up_weight,
    up_bias,
    down_weight,
    down_bias,
    cotangent,
):
    local_rows = tokens.shape[0]
    group_count = lax.axis_size("group")
    seq_rows = local_rows * group_count
    member = lax.axis_index("group")
    position = member * local_rows + jnp.arange(local_rows, dtype=jnp.int32)
    active = ((position < lengths[0]) & (exit_layers > LAYER)).astype(jnp.float32)[:, None]
    allowed = jnp.arange(seq_rows, dtype=jnp.int32)[None, :] <= position[:, None]
    (
        gain_one,
        shift_one,
        gain_two,
        shift_two,
        query_full,
        key_full,
        value_full,
        out_full,
        qbias_full,
        vbias_full,
        obias_full,
    ) = (
        lax.all_gather(pre_gain, "group", axis=0, tiled=True),
        lax.all_gather(pre_shift, "group", axis=0, tiled=True),
        lax.all_gather(mid_gain, "group", axis=0, tiled=True),
        lax.all_gather(mid_shift, "group", axis=0, tiled=True),
        lax.all_gather(query_weight, "group", axis=0, tiled=True),
        lax.all_gather(key_weight, "group", axis=0, tiled=True),
        lax.all_gather(value_weight, "group", axis=0, tiled=True),
        lax.all_gather(out_weight, "group", axis=0, tiled=True),
        lax.all_gather(query_bias, "group", axis=0, tiled=True),
        lax.all_gather(value_bias, "group", axis=0, tiled=True),
        lax.all_gather(out_bias, "group", axis=0, tiled=True),
    )
    inputs = tokens.astype(jnp.float32)
    normed_one, factor_one = layer_norm(inputs)
    attn_in = (normed_one * gain_one.astype(jnp.float32) + shift_one.astype(jnp.float32)).astype(
        jnp.bfloat16
    )
    queries = (matmul(attn_in, query_full) + qbias_full.astype(jnp.float32)).astype(jnp.bfloat16)
    keys_local = matmul(attn_in, key_full).astype(jnp.bfloat16)
    values_local = (matmul(attn_in, value_full) + vbias_full.astype(jnp.float32)).astype(
        jnp.bfloat16
    )
    keys_all, values_all = (
        lax.all_gather(keys_local, "group", axis=0, tiled=True),
        lax.all_gather(values_local, "group", axis=0, tiled=True),
    )
    query_heads = split_heads(queries)
    key_heads = split_heads(keys_all)
    value_heads = split_heads(values_all)

    def forward_group(operands):
        query_group, key_group, value_group = operands
        scores = score_block(query_group, key_group, allowed)
        top = jnp.max(scores, -1, keepdims=True)
        logsum = top + jnp.log(jnp.sum(jnp.exp(scores - top), -1, keepdims=True))
        weights = jnp.exp(scores - logsum).astype(jnp.bfloat16)
        context_part = jnp.einsum(
            "hqk,khd->qhd", weights, value_group, preferred_element_type=jnp.float32
        )
        return (context_part, logsum[..., 0])

    context_heads, logsums = lax.map(forward_group, (query_heads, key_heads, value_heads))
    context_low = join_heads(context_heads).astype(jnp.bfloat16)
    attn_out = matmul(context_low, out_full) + obias_full.astype(jnp.float32)
    hidden = inputs + active * attn_out
    normed_two, factor_two = layer_norm(hidden)
    ffn_in = (normed_two * gain_two.astype(jnp.float32) + shift_two.astype(jnp.float32)).astype(
        jnp.bfloat16
    )
    up_full, upbias_full, down_full, downbias_full = (
        lax.all_gather(up_weight, "group", axis=1, tiled=True),
        lax.all_gather(up_bias, "group", axis=0, tiled=True),
        lax.all_gather(down_weight, "group", axis=0, tiled=True),
        lax.all_gather(down_bias, "group", axis=0, tiled=True),
    )
    pre_act = matmul(ffn_in, up_full) + upbias_full.astype(jnp.float32)
    act_low = gelu(pre_act).astype(jnp.bfloat16)
    branch = matmul(act_low, down_full) + downbias_full.astype(jnp.float32)
    output = (hidden + active * branch).astype(jnp.bfloat16)
    first_gain, second_gain, query_back, key_back, value_back, out_back = (
        lax.all_gather(pre_gain, "group", axis=0, tiled=True),
        lax.all_gather(mid_gain, "group", axis=0, tiled=True),
        lax.all_gather(query_weight, "group", axis=0, tiled=True),
        lax.all_gather(key_weight, "group", axis=0, tiled=True),
        lax.all_gather(value_weight, "group", axis=0, tiled=True),
        lax.all_gather(out_weight, "group", axis=0, tiled=True),
    )
    grad_out = cotangent.astype(jnp.float32)
    branch_grad = (active * grad_out).astype(jnp.bfloat16)
    up_back, down_back = (
        lax.all_gather(up_weight, "group", axis=1, tiled=True),
        lax.all_gather(down_weight, "group", axis=0, tiled=True),
    )
    act_grad = matmul(branch_grad, down_back.T)
    pre_grad = gelu_back(pre_act, act_grad).astype(jnp.bfloat16)
    ffn_in_grad = matmul(pre_grad, up_back.T)
    up_grad, up_bias_grad, down_grad, down_bias_grad = (
        lax.psum_scatter(
            matmul(ffn_in.T, pre_grad).astype(jnp.bfloat16),
            "group",
            scatter_dimension=1,
            tiled=True,
        ).astype(jnp.float32),
        lax.psum_scatter(
            column_sums(pre_grad).astype(jnp.bfloat16), "group", scatter_dimension=0, tiled=True
        ).astype(jnp.float32),
        lax.psum_scatter(
            matmul(act_low.T, branch_grad).astype(jnp.bfloat16),
            "group",
            scatter_dimension=0,
            tiled=True,
        ).astype(jnp.float32),
        lax.psum_scatter(
            column_sums(branch_grad).astype(jnp.bfloat16), "group", scatter_dimension=0, tiled=True
        ).astype(jnp.float32),
    )
    mid_gain_part = jnp.sum(ffn_in_grad * normed_two, 0)
    mid_shift_part = jnp.sum(ffn_in_grad, 0)
    hidden_grad = grad_out + norm_back(
        ffn_in_grad * second_gain.astype(jnp.float32), normed_two, factor_two
    )
    attn_grad = (active * hidden_grad).astype(jnp.bfloat16)
    context_grad = matmul(attn_grad, out_back.T).astype(jnp.bfloat16)
    out_bias_part = column_sums(attn_grad)

    def backward_group(operands):
        query_group, key_group, value_group, grad_group, logsum_group = operands
        scores = score_block(query_group, key_group, allowed)
        probs = jnp.exp(scores - logsum_group[..., None])
        probs_grad = jnp.einsum(
            "qhd,khd->hqk", grad_group, value_group, preferred_element_type=jnp.float32
        )
        delta = jnp.sum(probs * probs_grad, -1, keepdims=True)
        score_grad = (probs * (probs_grad - delta)).astype(jnp.bfloat16)
        query_part = (
            jnp.einsum("hqk,khd->qhd", score_grad, key_group, preferred_element_type=jnp.float32)
            * 0.125
        )
        key_part = (
            jnp.einsum("hqk,qhd->khd", score_grad, query_group, preferred_element_type=jnp.float32)
            * 0.125
        )
        value_part = jnp.einsum(
            "hqk,qhd->khd",
            probs.astype(jnp.bfloat16),
            grad_group,
            preferred_element_type=jnp.float32,
        )
        return (query_part, key_part, value_part)

    query_parts, key_parts, value_parts = lax.map(
        backward_group, (query_heads, key_heads, value_heads, split_heads(context_grad), logsums)
    )
    query_grad = join_heads(query_parts).astype(jnp.bfloat16)
    key_sum, value_sum = (
        lax.psum_scatter(
            join_heads(key_parts).astype(jnp.bfloat16), "group", scatter_dimension=0, tiled=True
        ).astype(jnp.float32),
        lax.psum_scatter(
            join_heads(value_parts).astype(jnp.bfloat16), "group", scatter_dimension=0, tiled=True
        ).astype(jnp.float32),
    )
    key_grad = key_sum.astype(jnp.bfloat16)
    value_grad = value_sum.astype(jnp.bfloat16)
    in_grad = (
        matmul(query_grad, query_back.T)
        + matmul(key_grad, key_back.T)
        + matmul(value_grad, value_back.T)
    )
    pre_gain_part = jnp.sum(in_grad * normed_one, 0)
    pre_shift_part = jnp.sum(in_grad, 0)
    token_grad = (
        hidden_grad + norm_back(in_grad * first_gain.astype(jnp.float32), normed_one, factor_one)
    ).astype(jnp.bfloat16)
    (
        pre_gain_grad,
        pre_shift_grad,
        mid_gain_grad,
        mid_shift_grad,
        query_wgrad,
        key_wgrad,
        value_wgrad,
        out_wgrad,
        query_bgrad,
        value_bgrad,
        out_bgrad,
    ) = (
        lax.psum_scatter(
            pre_gain_part.astype(jnp.bfloat16), "group", scatter_dimension=0, tiled=True
        ).astype(jnp.float32),
        lax.psum_scatter(
            pre_shift_part.astype(jnp.bfloat16), "group", scatter_dimension=0, tiled=True
        ).astype(jnp.float32),
        lax.psum_scatter(
            mid_gain_part.astype(jnp.bfloat16), "group", scatter_dimension=0, tiled=True
        ).astype(jnp.float32),
        lax.psum_scatter(
            mid_shift_part.astype(jnp.bfloat16), "group", scatter_dimension=0, tiled=True
        ).astype(jnp.float32),
        lax.psum_scatter(
            matmul(attn_in.T, query_grad).astype(jnp.bfloat16),
            "group",
            scatter_dimension=0,
            tiled=True,
        ).astype(jnp.float32),
        lax.psum_scatter(
            matmul(attn_in.T, key_grad).astype(jnp.bfloat16),
            "group",
            scatter_dimension=0,
            tiled=True,
        ).astype(jnp.float32),
        lax.psum_scatter(
            matmul(attn_in.T, value_grad).astype(jnp.bfloat16),
            "group",
            scatter_dimension=0,
            tiled=True,
        ).astype(jnp.float32),
        lax.psum_scatter(
            matmul(context_low.T, attn_grad).astype(jnp.bfloat16),
            "group",
            scatter_dimension=0,
            tiled=True,
        ).astype(jnp.float32),
        lax.psum_scatter(
            column_sums(query_grad).astype(jnp.bfloat16), "group", scatter_dimension=0, tiled=True
        ).astype(jnp.float32),
        lax.psum_scatter(
            column_sums(value_grad).astype(jnp.bfloat16), "group", scatter_dimension=0, tiled=True
        ).astype(jnp.float32),
        lax.psum_scatter(
            out_bias_part.astype(jnp.bfloat16), "group", scatter_dimension=0, tiled=True
        ).astype(jnp.float32),
    )
    totals = (
        lax.psum(pre_gain_grad.astype(jnp.bfloat16), "replica").astype(jnp.float32),
        lax.psum(pre_shift_grad.astype(jnp.bfloat16), "replica").astype(jnp.float32),
        lax.psum(query_wgrad.astype(jnp.bfloat16), "replica").astype(jnp.float32),
        lax.psum(query_bgrad.astype(jnp.bfloat16), "replica").astype(jnp.float32),
        lax.psum(key_wgrad.astype(jnp.bfloat16), "replica").astype(jnp.float32),
        lax.psum(value_wgrad.astype(jnp.bfloat16), "replica").astype(jnp.float32),
        lax.psum(value_bgrad.astype(jnp.bfloat16), "replica").astype(jnp.float32),
        lax.psum(out_wgrad.astype(jnp.bfloat16), "replica").astype(jnp.float32),
        lax.psum(out_bgrad.astype(jnp.bfloat16), "replica").astype(jnp.float32),
        lax.psum(mid_gain_grad.astype(jnp.bfloat16), "replica").astype(jnp.float32),
        lax.psum(mid_shift_grad.astype(jnp.bfloat16), "replica").astype(jnp.float32),
        lax.psum(up_grad.astype(jnp.bfloat16), "replica").astype(jnp.float32),
        lax.psum(up_bias_grad.astype(jnp.bfloat16), "replica").astype(jnp.float32),
        lax.psum(down_grad.astype(jnp.bfloat16), "replica").astype(jnp.float32),
        lax.psum(down_bias_grad.astype(jnp.bfloat16), "replica").astype(jnp.float32),
    )
    return (
        output,
        token_grad,
        totals[0],
        totals[1],
        totals[2],
        totals[3],
        totals[4],
        totals[5],
        totals[6],
        totals[7],
        totals[8],
        totals[9],
        totals[10],
        totals[11],
        totals[12],
        totals[13],
        totals[14],
    )


def solution(mesh):
    return jax.shard_map(
        shards,
        mesh=mesh,
        in_specs=(
            P(("replica", "group"), None),
            P("replica"),
            P(("replica", "group")),
            P("group"),
            P("group"),
            P("group", None),
            P("group"),
            P("group", None),
            P("group", None),
            P("group"),
            P("group", None),
            P("group"),
            P("group"),
            P("group"),
            P(None, "group"),
            P("group"),
            P("group", None),
            P("group"),
            P(("replica", "group"), None),
        ),
        out_specs=(
            P(("replica", "group"), None),
            P(("replica", "group"), None),
            P("group"),
            P("group"),
            P("group", None),
            P("group"),
            P("group", None),
            P("group", None),
            P("group"),
            P("group", None),
            P("group"),
            P("group"),
            P("group"),
            P(None, "group"),
            P("group"),
            P("group", None),
            P("group"),
        ),
        check_vma=False,
    )
```

profile of v0, /device:TPU:0, one launch (start us, length us, event | category | flops | bytes accessed | tf_op | source)
XLA Modules:
  0.0 2687.4 jit_solution(7998907598796842740)
XLA Ops:
  34.8 65.6 %all-gather.17.cloned.1.call-done = bf16[2048,2048]{1,0:T(8,128)(2,1)} async-done(((bf16[512,2048]{1,0:T(8,128)(2,1)}), bf16[2048,2048]{1,0:T(8,128)(2,1)}) %all-gather.17.cloned.1.call-update) | async-done | bytes 8388624 | tf_op jit(solution)/shard_map/all_gather | solution.py:116
  105.9 83.9 %all-gather.23.cloned.1.call-done = bf16[2048,2048]{1,0:T(8,128)(2,1)} async-done(((bf16[512,2048]{1,0:T(8,128)(2,1)}), bf16[2048,2048]{1,0:T(8,128)(2,1)}) %all-gather.23.cloned.1.call-update) | async-done | bytes 8388624 | tf_op jit(solution)/shard_map/all_gather | solution.py:115
  237.1 42.5 %all-gather.21.cloned.1.call-done = bf16[2048,2048]{1,0:T(8,128)(2,1)} async-done(((bf16[512,2048]{1,0:T(8,128)(2,1)}), bf16[2048,2048]{1,0:T(8,128)(2,1)}) %all-gather.21.cloned.1.call-update) | async-done | bytes 8388624 | tf_op jit(solution)/shard_map/all_gather | solution.py:114
  284.6 32.6 %all-gather.19.cloned.1.call-done = bf16[512,2048]{1,0:T(8,128)(2,1)} async-done(((bf16[128,2048]{1,0:T(8,128)(2,1)}), bf16[512,2048]{1,0:T(8,128)(2,1)}) %all-gather.19.cloned.1.call-update) | async-done | bytes 2097168 | tf_op jit(solution)/shard_map/all_gather | solution.py:134
  321.3 33.5 %all-gather.25.cloned.1.call-done = bf16[512,2048]{1,0:T(8,128)(2,1)} async-done(((bf16[128,2048]{1,0:T(8,128)(2,1)}), bf16[512,2048]{1,0:T(8,128)(2,1)}) %all-gather.25.cloned.1.call-update) | async-done | bytes 2097168 | tf_op jit(solution)/shard_map/all_gather | solution.py:133
  374.4 69.8 %all-gather.27.cloned.1.call-done = bf16[2048,2048]{1,0:T(8,128)(2,1)} async-done(((bf16[512,2048]{1,0:T(8,128)(2,1)}), bf16[2048,2048]{1,0:T(8,128)(2,1)}) %all-gather.27.cloned.1.call-update) | async-done | bytes 8388624 | tf_op jit(solution)/shard_map/all_gather | solution.py:117
  450.3 292.9 %all-gather.29.cloned.1.call-done = bf16[2048,8192]{1,0:T(8,128)(2,1)} async-done(((bf16[2048,2048]{1,0:T(8,128)(2,1)}), bf16[2048,8192]{1,0:T(8,128)(2,1)}) %all-gather.29.cloned.1.call-update) | async-done | bytes 33554448 | tf_op jit(solution)/shard_map/all_gather | solution.py:160
  743.3 20.8 convolution_add_fusion
  764.0 278.3 %all-gather.31.cloned.1.call-done = bf16[8192,2048]{1,0:T(8,128)(2,1)} async-done(((bf16[2048,2048]{1,0:T(8,128)(2,1)}), bf16[8192,2048]{1,0:T(8,128)(2,1)}) %all-gather.31.cloned.1.call-update) | async-done | bytes 33554448 | tf_op jit(solution)/shard_map/all_gather | solution.py:162
  1042.3 18.8 fusion.81
  1061.2 19.7 multiply_reduce_fusion.1
  1095.0 31.3 %while.29 = (s32[]{:T(128)}, bf16[4,128,8,64]{1,3,2,0:T(8,128)(2,1)}, bf16[4,512,8,64]{1,3,2,0:T(8,128)(2,1)}, bf16[4,512,8,64]{1,3,2,0:T(8,128)(2,1)}, bf16[4,5...) while((s32[]{:T(128)}, ...), condition=%wide.region_12.13_spmd.clone, body=%wide.region_10.12_spmd.clone.sunk | while | flops 340655104 | bytes 58091296 | solution.py:240
  1147.0 18.6 reduce-scatter.25.cloned.1.call-done
  1172.5 31.9 %reduce-scatter.27.cloned.1.call-done = bf16[128,2048]{1,0:T(8,128)(2,1)} async-done(((bf16[512,2048]{1,0:T(8,128)(2,1)}), bf16[128,2048]{1,0:T(8,128)(2,1)}) %reduce-scatter.27.cloned.1.call-update) | async-done | bytes 524304
  1229.1 16.6 convolution_convert_fusion.1
  1245.8 48.8 %reduce-scatter.15.cloned.1.call-done = bf16[512,2048]{1,0:T(8,128)(2,1)} async-done(((bf16[2048,2048]{1,0:T(8,128)(2,1)}), bf16[512,2048]{1,0:T(8,128)(2,1)}) %reduce-scatter.15.cloned.1.call-update) | async-done | bytes 2097168 | tf_op jit(solution)/shard_map/reduce_scatter | solution.py:289
  1294.5 89.6 %reduce-scatter.21.cloned.1.call-done = bf16[512,2048]{1,0:T(8,128)(2,1)} async-done(((bf16[2048,2048]{1,0:T(8,128)(2,1)}), bf16[512,2048]{1,0:T(8,128)(2,1)}) %reduce-scatter.21.cloned.1.call-update) | async-done | bytes 2097168 | tf_op jit(solution)/shard_map/reduce_scatter | solution.py:307
  1384.2 90.1 %reduce-scatter.17.cloned.1.call-done = bf16[512,2048]{1,0:T(8,128)(2,1)} async-done(((bf16[2048,2048]{1,0:T(8,128)(2,1)}), bf16[512,2048]{1,0:T(8,128)(2,1)}) %reduce-scatter.17.cloned.1.call-update) | async-done | bytes 2097168 | tf_op jit(solution)/shard_map/reduce_scatter | solution.py:295
  1474.2 89.6 %reduce-scatter.19.cloned.1.call-done = bf16[512,2048]{1,0:T(8,128)(2,1)} async-done(((bf16[2048,2048]{1,0:T(8,128)(2,1)}), bf16[512,2048]{1,0:T(8,128)(2,1)}) %reduce-scatter.19.cloned.1.call-update) | async-done | bytes 2097168 | tf_op jit(solution)/shard_map/reduce_scatter | solution.py:301
  1563.9 291.6 %reduce-scatter.23.cloned.1.call-done = bf16[2048,2048]{1,0:T(8,128)(2,1)} async-done(((bf16[2048,8192]{1,0:T(8,128)(2,1)}), bf16[2048,2048]{1,0:T(8,128)(2,1)}) %reduce-scatter.23.cloned.1.call-update) | async-done | bytes 8388624 | tf_op jit(solution)/shard_map/reduce_scatter | solution.py:187
  1855.5 291.9 %reduce-scatter.29.cloned.1.call-done = bf16[2048,2048]{1,0:T(8,128)(2,1)} async-done(((bf16[8192,2048]{1,0:T(8,128)(2,1)}), bf16[2048,2048]{1,0:T(8,128)(2,1)}) %reduce-scatter.29.cloned.1.call-update) | async-done | bytes 8388624
  2164.9 18.0 fusion.52
  2213.1 28.0 %all-reduce.10 = (bf16[512]{0:T(512)(128)(2,1)S(1)}, bf16[512]{0:T(512)(128)(2,1)S(1)}, bf16[512]{0:T(512)(128)(2,1)S(1)}, bf16[512]{0:T(512)(128)(2,1)S(1)}, bf...) all-reduce(bf16[512]{0:T(512)(128)(2,1)S(1)} %dynamic-slice.1, ...), channel_id=1, replica_groups=mesh['replica'=8,'group'=4] {'replica'}, use_global_device_ids=true, to_apply=%region_19.20 | all-reduce | flops 6144 | bytes 24576 | tf_op jit(solution)/shard_map/psum | solution.py:324
  2247.6 397.6 %all-reduce.15.cloned.1.call-done = (bf16[512,2048]{1,0:T(8,128)(2,1)}, bf16[512,2048]{1,0:T(8,128)(2,1)}, bf16[512,2048]{1,0:T(8,128)(2,1)}, bf16[512,2048]{1,0...) async-done(((bf16[512,2048]{1,0:T(8,128)(2,1)}, bf16[512,2048]{1,0:T(8,128)(2,1)}, bf16[512,2048]{1,0:T(8,128)(2,1)}, bf16[512,2048]{1,0:T(8,128)(2,1)}, ...) | async-done | bytes 25165840 | tf_op jit(solution)/shard_map/psum | solution.py:326
  (292 shorter events, 315.1 us)
Async XLA Ops:
  7.2 19.9 copy-start.24
  7.2 27.1 %copy-start = (bf16[128,2048]{1,0:T(8,128)(2,1)S(1)}, bf16[128,2048]{1,0:T(8,128)(2,1)}, u32[]{:S(2)}) copy-start(bf16[128,2048]{1,0:T(8,128)(2,1)} %param.23) | copy-start | bytes 1572868
  7.2 93.1 %all-gather.17.cloned.1.call-start = ((), (), s32[]{:S(2)}) async-start(), calls=%async_computation.8 | async-start | bytes 10485760 | tf_op jit(solution)/shard_map/all_gather | solution.py:116
  8.0 181.9 %all-gather.23.cloned.1.call-start = ((), (), s32[]{:S(2)}) async-start(), calls=%async_computation.11 | async-start | bytes 10485760 | tf_op jit(solution)/shard_map/all_gather | solution.py:115
  8.7 270.9 %all-gather.21.cloned.1.call-start = ((), (), s32[]{:S(2)}) async-start(), calls=%async_computation.10 | async-start | bytes 10485760 | tf_op jit(solution)/shard_map/all_gather | solution.py:114
  9.4 307.7 %all-gather.19.cloned.1.call-start = ((), (), s32[]{:S(2)}) async-start(), calls=%async_computation.9 | async-start | bytes 2621440 | tf_op jit(solution)/shard_map/all_gather | solution.py:134
  105.9 248.9 %all-gather.25.cloned.1.call-start = ((), (), s32[]{:S(2)}) async-start(), calls=%async_computation.12 | async-start | bytes 2621440 | tf_op jit(solution)/shard_map/all_gather | solution.py:133
  195.4 248.8 %all-gather.27.cloned.1.call-start = ((), (), s32[]{:S(2)}) async-start(), calls=%async_computation.13 | async-start | bytes 10485760 | tf_op jit(solution)/shard_map/all_gather | solution.py:117
  195.9 547.3 %all-gather.29.cloned.1.call-start = ((), (), s32[]{:S(2)}) async-start(), calls=%async_computation.14 | async-start | bytes 41943040 | tf_op jit(solution)/shard_map/all_gather | solution.py:160
  196.7 25.1 copy-start.27
  196.7 32.2 %copy-start.28 = (bf16[512]{0:T(512)(128)(2,1)S(1)}, bf16[512]{0:T(512)(128)(2,1)}, u32[]{:S(2)}) copy-start(bf16[512]{0:T(512)(128)(2,1)} %param.35) | copy-start | bytes 3076
  196.7 40.3 %copy-start.30 = (s32[128]{0:T(128)S(1)}, s32[128]{0:T(128)}, u32[]{:S(2)}) copy-start(s32[128]{0:T(128)} %param.25) | copy-start | bytes 1540
  196.8 845.6 %all-gather.31.cloned.1.call-start = ((), (), s32[]{:S(2)}) async-start(), calls=%async_computation.15 | async-start | bytes 41943040 | tf_op jit(solution)/shard_map/all_gather | solution.py:162
  197.5 968.0 %reduce-scatter.25.cloned.1.call-start = ((), (), s32[]{:S(2)}) async-start(), calls=%async_computation.21 | async-start | bytes 2621440
  1130.2 74.2 %reduce-scatter.27.cloned.1.call-start = ((), (), s32[]{:S(2)}) async-start(), calls=%async_computation.22 | async-start | bytes 2621440
  1134.2 160.3 %reduce-scatter.15.cloned.1.call-start = ((), (), s32[]{:S(2)}) async-start(), calls=%async_computation.16 | async-start | bytes 10485760 | tf_op jit(solution)/shard_map/reduce_scatter | solution.py:289
  1140.2 244.0 %reduce-scatter.21.cloned.1.call-start = ((), (), s32[]{:S(2)}) async-start(), calls=%async_computation.19 | async-start | bytes 10485760 | tf_op jit(solution)/shard_map/reduce_scatter | solution.py:307
  1146.9 327.3 %reduce-scatter.17.cloned.1.call-start = ((), (), s32[]{:S(2)}) async-start(), calls=%async_computation.17 | async-start | bytes 10485760 | tf_op jit(solution)/shard_map/reduce_scatter | solution.py:295
  1172.5 391.4 %reduce-scatter.19.cloned.1.call-start = ((), (), s32[]{:S(2)}) async-start(), calls=%async_computation.18 | async-start | bytes 10485760 | tf_op jit(solution)/shard_map/reduce_scatter | solution.py:301
  1211.2 644.3 %reduce-scatter.23.cloned.1.call-start = ((), (), s32[]{:S(2)}) async-start(), calls=%async_computation.20 | async-start | bytes 41943040 | tf_op jit(solution)/shard_map/reduce_scatter | solution.py:187
  1228.1 919.2 %reduce-scatter.29.cloned.1.call-start = ((), (), s32[]{:S(2)}) async-start(), calls=%async_computation.23 | async-start | bytes 41943040
  1245.7 1399.5 %all-reduce.15.cloned.1.call-start = ((), (), s32[]{:S(2)}) async-start(), calls=%async_computation.24 | async-start | bytes 50331648 | tf_op jit(solution)/shard_map/psum | solution.py:326
  2164.8 18.1 copy-start.9
  2189.5 56.9 %copy-start.12 = (f32[128,2048]{1,0:T(8,128)S(1)}, f32[128,2048]{1,0:T(8,128)}, u32[]{:S(2)}) copy-start(f32[128,2048]{1,0:T(8,128)} %get-tuple-element.224) | copy-start | bytes 3145732
  (49 other events, 125.0 us)
Sparse Core Ops, SparseCore 0:
  9.9 90.3 all-gather.16
  102.2 87.5 all-gather.22
  191.7 87.8 all-gather.20
  281.8 35.3 all-gather.18
  319.5 35.2 all-gather.24
  356.5 87.5 all-gather.26
  446.0 297.2 all-gather.28
  745.1 297.2 all-gather.30
  1130.3 35.1 reduce-scatter.24
  1169.2 35.1 reduce-scatter.26
  1208.1 86.3 reduce-scatter.14
  1297.7 86.3 reduce-scatter.20
  1387.8 86.3 reduce-scatter.16
  1477.4 86.3 reduce-scatter.18
  1566.8 288.6 reduce-scatter.22
  1858.7 288.6 reduce-scatter.28
  2150.5 494.6 all-reduce.14
where the time goes:
time: 2690 us
  waiting for transfers between devices  2250 us (84%)
  matrix products  210 us (8%)
  blocking collectives  116 us (4%)
  other arithmetic  50.9 us (2%)
  local copies, waits for them, and re-layouts  39.5 us (1%)
    psum x1, waiting for transfers between devices, shards(): lax.psum(query_wgrad.astype(jnp.bfloat16), 'replica').astype(jnp.float32)  398 us
    unnamed x20, waiting for transfers between devices  346 us
    all_gather x1, waiting for transfers between devices, shards(): lax.all_gather(up_weight, 'group', axis=1, tiled=True)  293 us
    reduce_scatter x1, waiting for transfers between devices, shards(): lax.psum_scatter(matmul(ffn_in.T, pre_grad).astype(jnp.bfloat16), 'group'...  292 us
    all_gather x1, waiting for transfers between devices, shards(): lax.all_gather(down_weight, 'group', axis=0, tiled=True)  278 us
    dot_general x18, matrix products, matmul(): return jnp.dot(left, right, preferred_element_type=jnp.float32)  182 us
    reduce_scatter x1, waiting for transfers between devices, shards(): lax.psum_scatter(matmul(attn_in.T, key_grad).astype(jnp.bfloat16), 'group...  90.1 us
    reduce_scatter x1, waiting for transfers between devices, shards(): lax.psum_scatter(matmul(attn_in.T, value_grad).astype(jnp.bfloat16), 'gro...  89.6 us
  transfers between devices with their start and end apart: 17, of which 17 were waited for; matrix products, arithmetic and copies ran while one was open for 6% of the time, Pallas kernels for 0%

commit v1 on v0

--- a/solution.py
+++ b/solution.py
@@ -7,6 +7,19 @@
 H = 32
 HD = 64
 LAYER = 12
+
+
+def gather_around(shard, axis, dim):
+    ways = lax.axis_size(axis)
+    up = [(d, (d + 1) % ways) for d in range(ways)]
+    down = [(d, (d - 1) % ways) for d in range(ways)]
+    earlier, later = ([shard], [shard])
+    for _ in range(ways // 2):
+        earlier.append(lax.ppermute(earlier[-1], axis, up))
+    for _ in range((ways - 1) // 2):
+        later.append(lax.ppermute(later[-1], axis, down))
+    line = jnp.concatenate([*earlier[::-1], *later[1:]], axis=dim)
+    return jnp.roll(line, (lax.axis_index(axis) - ways // 2) * shard.shape[dim], axis=dim)
 
 
 def layer_norm(values):
@@ -113,7 +126,7 @@
         lax.all_gather(mid_shift, "group", axis=0, tiled=True),
         lax.all_gather(query_weight, "group", axis=0, tiled=True),
         lax.all_gather(key_weight, "group", axis=0, tiled=True),
-        lax.all_gather(value_weight, "group", axis=0, tiled=True),
+        gather_around(value_weight, "group", 0),
         lax.all_gather(out_weight, "group", axis=0, tiled=True),
         lax.all_gather(query_bias, "group", axis=0, tiled=True),
         lax.all_gather(value_bias, "group", axis=0, tiled=True),

time: 2690 us -> 2840 us (1.056)
  blocking collectives: 116 us -> 236 us
    all_gather x1, blocking collectives: 9.52 us -> 130 us  [shards(): lax.all_gather(value_bias, 'group', axis=0, tiled=True)]
    all_gather x1, waiting for transfers between devices: 83.9 us -> 0.02 us  [shards(): lax.all_gather(key_weight, 'group', axis=0, tiled=True)]
    ppermute x0 -> x3, waiting for transfers between devices: none -> 72.5 us  [the longest x2 72.5 us: gather_around(): earlier.append(lax.ppermute(earlier[-1], axis, up))]
    psum x1, waiting for transfers between devices: 398 us -> 440 us  [shards(): lax.psum(query_wgrad.astype(jnp.bfloat16), 'replica').astype(jnp.float32)]
    all_gather x1, waiting for transfers between devices: 32.6 us -> 0.02 us  [shards(): lax.all_gather(values_local, 'group', axis=0, tiled=True)]
    all_gather x1, waiting for transfers between devices: 42.5 us -> 73.2 us  [shards(): lax.all_gather(query_weight, 'group', axis=0, tiled=True)]
  transfers between devices with their start and end apart: 17 -> 20, of which waited for: 17 -> 16; matrix products, arithmetic and copies ran while one was open for 6% -> 6% of each run, Pallas kernels for 0% -> 0%
where the time goes in v1:
time: 2840 us; the launch traced here: 2830 us
  waiting for transfers between devices  2260 us (80%)
  blocking collectives  236 us (8%)
  matrix products  208 us (7%)
  other arithmetic  53 us (2%)
  local copies, waits for them, and re-layouts  50.1 us (2%)
    psum x1, waiting for transfers between devices, shards(): lax.psum(query_wgrad.astype(jnp.bfloat16), 'replica').astype(jnp.float32)  440 us
    unnamed x20, waiting for transfers between devices  346 us
    all_gather x1, waiting for transfers between devices, shards(): lax.all_gather(up_weight, 'group', axis=1, tiled=True)  293 us
    reduce_scatter x1, waiting for transfers between devices, shards(): lax.psum_scatter(matmul(ffn_in.T, pre_grad).astype(jnp.bfloat16), 'group'...  292 us
    all_gather x1, waiting for transfers between devices, shards(): lax.all_gather(down_weight, 'group', axis=0, tiled=True)  278 us
    dot_general x18, matrix products, matmul(): return jnp.dot(left, right, preferred_element_type=jnp.float32)  180 us
    all_gather x1, blocking collectives, shards(): lax.all_gather(value_bias, 'group', axis=0, tiled=True)  130 us
    reduce_scatter x1, waiting for transfers between devices, shards(): lax.psum_scatter(matmul(attn_in.T, key_grad).astype(jnp.bfloat16), 'group...  89.9 us
  transfers between devices with their start and end apart: 20, of which 16 were waited for; matrix products, arithmetic and copies ran while one was open for 6% of the time, Pallas kernels for 0%

profile of v1, /device:TPU:0, one launch (start us, length us, event | category | flops | bytes accessed | tf_op | source)
XLA Modules:
  0.0 2832.2 jit_solution(7306997428938926380)
XLA Ops:
  11.0 72.5 %collective-permute-done = bf16[512,2048]{1,0:T(8,128)(2,1)S(1)} collective-permute-done((bf16[512,2048]{1,0:T(8,128)(2,1)}, bf16[512,2048]{1,0:T(8,128)(2,1)S(1)}, u32[]{:S(2)}, u32[]{:S(2)}) %collective-permute-start) | collective-permute-done | bytes 2097184 | tf_op jit(solution)/shard_map/ppermute | solution.py:18
  87.3 130.2 %all-gather.2 = bf16[4,1,512]{2,1,0:T(2,128)(2,1)S(1)} all-gather(bf16[1,1,512]{2,1,0:T(2,128)(2,1)S(1)} %reshape.148), channel_id=1, replica_groups=mesh['replica'=8,'group'=4] {'group'}, dimensions={0}, use_global_device_ids=true | all-gather | bytes 5120 | tf_op jit(solution)/shard_map/all_gather | solution.py:132
  299.3 73.2 %all-gather.19.cloned.1.call-done = bf16[2048,2048]{1,0:T(8,128)(2,1)} async-done(((bf16[512,2048]{1,0:T(8,128)(2,1)}), bf16[2048,2048]{1,0:T(8,128)(2,1)}) %all-gather.19.cloned.1.call-update) | async-done | bytes 8388624 | tf_op jit(solution)/shard_map/all_gather | solution.py:127
  377.5 32.6 %all-gather.23.cloned.1.call-done = bf16[512,2048]{1,0:T(8,128)(2,1)} async-done(((bf16[128,2048]{1,0:T(8,128)(2,1)}), bf16[512,2048]{1,0:T(8,128)(2,1)}) %all-gather.23.cloned.1.call-update) | async-done | bytes 2097168 | tf_op jit(solution)/shard_map/all_gather | solution.py:146
  429.7 69.7 %all-gather.25.cloned.1.call-done = bf16[2048,2048]{1,0:T(8,128)(2,1)} async-done(((bf16[512,2048]{1,0:T(8,128)(2,1)}), bf16[2048,2048]{1,0:T(8,128)(2,1)}) %all-gather.25.cloned.1.call-update) | async-done | bytes 8388624 | tf_op jit(solution)/shard_map/all_gather | solution.py:130
  505.8 292.7 %all-gather.27.cloned.1.call-done = bf16[2048,8192]{1,0:T(8,128)(2,1)} async-done(((bf16[2048,2048]{1,0:T(8,128)(2,1)}), bf16[2048,8192]{1,0:T(8,128)(2,1)}) %all-gather.27.cloned.1.call-update) | async-done | bytes 33554448 | tf_op jit(solution)/shard_map/all_gather | solution.py:173
  798.5 20.8 convolution_add_fusion
  819.2 278.3 %all-gather.29.cloned.1.call-done = bf16[8192,2048]{1,0:T(8,128)(2,1)} async-done(((bf16[2048,2048]{1,0:T(8,128)(2,1)}), bf16[8192,2048]{1,0:T(8,128)(2,1)}) %all-gather.29.cloned.1.call-update) | async-done | bytes 33554448 | tf_op jit(solution)/shard_map/all_gather | solution.py:175
  1097.5 19.3 fusion.89
  1116.8 19.3 multiply_reduce_fusion.1
  1150.3 31.3 %while.29 = (s32[]{:T(128)}, bf16[4,128,8,64]{1,3,2,0:T(8,128)(2,1)}, bf16[4,512,8,64]{1,3,2,0:T(8,128)(2,1)}, bf16[4,512,8,64]{1,3,2,0:T(8,128)(2,1)}, bf16[4,5...) while((s32[]{:T(128)}, ...), condition=%wide.region_12.13_spmd.clone, body=%wide.region_10.12_spmd.clone.sunk | while | flops 340655104 | bytes 58091296 | solution.py:253
  1202.4 18.4 reduce-scatter.25.cloned.1.call-done
  1227.8 32.1 %reduce-scatter.27.cloned.1.call-done = bf16[128,2048]{1,0:T(8,128)(2,1)} async-done(((bf16[512,2048]{1,0:T(8,128)(2,1)}), bf16[128,2048]{1,0:T(8,128)(2,1)}) %reduce-scatter.27.cloned.1.call-update) | async-done | bytes 524304
  1284.6 16.5 convolution_convert_fusion.1
  1301.7 48.1 %reduce-scatter.15.cloned.1.call-done = bf16[512,2048]{1,0:T(8,128)(2,1)} async-done(((bf16[2048,2048]{1,0:T(8,128)(2,1)}), bf16[512,2048]{1,0:T(8,128)(2,1)}) %reduce-scatter.15.cloned.1.call-update) | async-done | bytes 2097168 | tf_op jit(solution)/shard_map/reduce_scatter | solution.py:302
  1349.8 89.8 %reduce-scatter.21.cloned.1.call-done = bf16[512,2048]{1,0:T(8,128)(2,1)} async-done(((bf16[2048,2048]{1,0:T(8,128)(2,1)}), bf16[512,2048]{1,0:T(8,128)(2,1)}) %reduce-scatter.21.cloned.1.call-update) | async-done | bytes 2097168 | tf_op jit(solution)/shard_map/reduce_scatter | solution.py:320
  1439.6 89.9 %reduce-scatter.17.cloned.1.call-done = bf16[512,2048]{1,0:T(8,128)(2,1)} async-done(((bf16[2048,2048]{1,0:T(8,128)(2,1)}), bf16[512,2048]{1,0:T(8,128)(2,1)}) %reduce-scatter.17.cloned.1.call-update) | async-done | bytes 2097168 | tf_op jit(solution)/shard_map/reduce_scatter | solution.py:308
  1529.5 89.8 %reduce-scatter.19.cloned.1.call-done = bf16[512,2048]{1,0:T(8,128)(2,1)} async-done(((bf16[2048,2048]{1,0:T(8,128)(2,1)}), bf16[512,2048]{1,0:T(8,128)(2,1)}) %reduce-scatter.19.cloned.1.call-update) | async-done | bytes 2097168 | tf_op jit(solution)/shard_map/reduce_scatter | solution.py:314
  1619.3 291.6 %reduce-scatter.23.cloned.1.call-done = bf16[2048,2048]{1,0:T(8,128)(2,1)} async-done(((bf16[2048,8192]{1,0:T(8,128)(2,1)}), bf16[2048,2048]{1,0:T(8,128)(2,1)}) %reduce-scatter.23.cloned.1.call-update) | async-done | bytes 8388624 | tf_op jit(solution)/shard_map/reduce_scatter | solution.py:200
  1910.9 291.9 %reduce-scatter.29.cloned.1.call-done = bf16[2048,2048]{1,0:T(8,128)(2,1)} async-done(((bf16[8192,2048]{1,0:T(8,128)(2,1)}), bf16[2048,2048]{1,0:T(8,128)(2,1)}) %reduce-scatter.29.cloned.1.call-update) | async-done | bytes 8388624
  2221.0 17.8 fusion.59
  2246.3 45.8 %all-gather.31.cloned.1.call-done = bf16[2048,2048]{1,0:T(8,128)(2,1)} async-done(((bf16[512,2048]{1,0:T(8,128)(2,1)}), bf16[2048,2048]{1,0:T(8,128)(2,1)}) %all-gather.31.cloned.1.call-update) | async-done | bytes 8388624 | tf_op jit(solution)/shard_map/all_gather | solution.py:187
  2315.6 28.0 all-reduce.10
  2350.1 439.9 %all-reduce.15.cloned.1.call-done = (bf16[512,2048]{1,0:T(8,128)(2,1)}, bf16[512,2048]{1,0:T(8,128)(2,1)}, bf16[512,2048]{1,0:T(8,128)(2,1)}, bf16[512,2048]{1,0...) async-done(((bf16[512,2048]{1,0:T(8,128)(2,1)}, bf16[512,2048]{1,0:T(8,128)(2,1)}, bf16[512,2048]{1,0:T(8,128)(2,1)}, bf16[512,2048]{1,0:T(8,128)(2,1)}, ...) | async-done | bytes 25165840 | tf_op jit(solution)/shard_map/psum | solution.py:339
  (302 shorter events, 322.3 us)
Async XLA Ops:
  7.2 240.6 %all-gather.21.cloned.1.call-start = ((), (), s32[]{:S(2)}) async-start(), calls=%async_computation.10 | async-start | bytes 10485760 | tf_op jit(solution)/shard_map/all_gather | solution.py:128
  7.9 287.2 %all-gather.17.cloned.1.call-start = ((), (), s32[]{:S(2)}) async-start(), calls=%async_computation.8 | async-start | bytes 2621440 | tf_op jit(solution)/shard_map/all_gather | solution.py:147
  8.0 75.5 %collective-permute-start = (bf16[512,2048]{1,0:T(8,128)(2,1)}, bf16[512,2048]{1,0:T(8,128)(2,1)S(1)}, u32[]{:S(2)}, u32[]{:S(2)}) collective-permute-start(bf16[512,2048]{1,0:T(8,128)(2,1)} %param.31), channel_id=1, source_target_pairs={{0,1},{1,2},{2,3},{3,0},{4,5},{5,6},{6,7},{7,4},{8,9},{9,10},{10,1... | collective-permute-start | bytes 6291464 | tf_op jit(solution)/shard_map/ppermute | solution.py:18
  83.5 153.1 %collective-permute-start.1 = (bf16[512,2048]{1,0:T(8,128)(2,1)S(1)}, bf16[512,2048]{1,0:T(8,128)(2,1)}, u32[]{:S(2)}, u32[]{:S(2)}) collective-permute-start(bf16[512,2048]{1,0:T(8,128)(2,1)S(1)} %collective-permute-done), channel_id=1, source_target_pairs={{0,1},{1,2},{2,3},{3,0},{4,5},{5,6},{6,7},{7,4},{8,9},{9,10},{10,1... | collective-permute-start | bytes 6291464 | tf_op jit(solution)/shard_map/ppermute | solution.py:18
  85.9 153.2 %collective-permute-start.2 = (bf16[512,2048]{1,0:T(8,128)(2,1)}, bf16[512,2048]{1,0:T(8,128)(2,1)}, u32[]{:S(2)}, u32[]{:S(2)}) collective-permute-start(bf16[512,2048]{1,0:T(8,128)(2,1)} %param.31), channel_id=1, source_target_pairs={{0,3},{1,0},{2,1},{3,2},{4,7},{5,4},{6,5},{7,6},{8,11},{9,8},{10,9... | collective-permute-start | bytes 6291464 | tf_op jit(solution)/shard_map/ppermute | solution.py:20
  247.0 125.5 %all-gather.19.cloned.1.call-start = ((), (), s32[]{:S(2)}) async-start(), calls=%async_computation.9 | async-start | bytes 10485760 | tf_op jit(solution)/shard_map/all_gather | solution.py:127
  247.8 162.4 %all-gather.23.cloned.1.call-start = ((), (), s32[]{:S(2)}) async-start(), calls=%async_computation.11 | async-start | bytes 2621440 | tf_op jit(solution)/shard_map/all_gather | solution.py:146
  253.4 246.1 %all-gather.25.cloned.1.call-start = ((), (), s32[]{:S(2)}) async-start(), calls=%async_computation.12 | async-start | bytes 10485760 | tf_op jit(solution)/shard_map/all_gather | solution.py:130
  253.9 544.5 %all-gather.27.cloned.1.call-start = ((), (), s32[]{:S(2)}) async-start(), calls=%async_computation.13 | async-start | bytes 41943040 | tf_op jit(solution)/shard_map/all_gather | solution.py:173
  254.6 25.1 copy-start.25
  254.6 32.2 %copy-start.26 = (bf16[512]{0:T(512)(128)(2,1)S(1)}, bf16[512]{0:T(512)(128)(2,1)}, u32[]{:S(2)}) copy-start(bf16[512]{0:T(512)(128)(2,1)} %param.35) | copy-start | bytes 3076
  254.6 40.5 %copy-start.28 = (s32[128]{0:T(128)S(1)}, s32[128]{0:T(128)}, u32[]{:S(2)}) copy-start(s32[128]{0:T(128)} %param.25) | copy-start | bytes 1540
  254.6 842.9 %all-gather.29.cloned.1.call-start = ((), (), s32[]{:S(2)}) async-start(), calls=%async_computation.14 | async-start | bytes 41943040 | tf_op jit(solution)/shard_map/all_gather | solution.py:175
  255.3 965.5 %reduce-scatter.25.cloned.1.call-start = ((), (), s32[]{:S(2)}) async-start(), calls=%async_computation.21 | async-start | bytes 2621440
  1185.5 74.4 %reduce-scatter.27.cloned.1.call-start = ((), (), s32[]{:S(2)}) async-start(), calls=%async_computation.22 | async-start | bytes 2621440
  1189.6 160.2 %reduce-scatter.15.cloned.1.call-start = ((), (), s32[]{:S(2)}) async-start(), calls=%async_computation.16 | async-start | bytes 10485760 | tf_op jit(solution)/shard_map/reduce_scatter | solution.py:302
  1195.6 244.0 %reduce-scatter.21.cloned.1.call-start = ((), (), s32[]{:S(2)}) async-start(), calls=%async_computation.19 | async-start | bytes 10485760 | tf_op jit(solution)/shard_map/reduce_scatter | solution.py:320
  1202.3 327.2 %reduce-scatter.17.cloned.1.call-start = ((), (), s32[]{:S(2)}) async-start(), calls=%async_computation.17 | async-start | bytes 10485760 | tf_op jit(solution)/shard_map/reduce_scatter | solution.py:308
  1227.8 391.5 %reduce-scatter.19.cloned.1.call-start = ((), (), s32[]{:S(2)}) async-start(), calls=%async_computation.18 | async-start | bytes 10485760 | tf_op jit(solution)/shard_map/reduce_scatter | solution.py:314
  1266.7 644.2 %reduce-scatter.23.cloned.1.call-start = ((), (), s32[]{:S(2)}) async-start(), calls=%async_computation.20 | async-start | bytes 41943040 | tf_op jit(solution)/shard_map/reduce_scatter | solution.py:200
  1283.6 919.2 %reduce-scatter.29.cloned.1.call-start = ((), (), s32[]{:S(2)}) async-start(), calls=%async_computation.23 | async-start | bytes 41943040
  1301.1 991.0 %all-gather.31.cloned.1.call-start = ((), (), s32[]{:S(2)}) async-start(), calls=%async_computation.15 | async-start | bytes 10485760 | tf_op jit(solution)/shard_map/all_gather | solution.py:187
  1301.7 1488.3 %all-reduce.15.cloned.1.call-start = ((), (), s32[]{:S(2)}) async-start(), calls=%async_computation.24 | async-start | bytes 50331648 | tf_op jit(solution)/shard_map/psum | solution.py:339
  2246.3 102.5 %copy-start.13 = (f32[128,2048]{1,0:T(8,128)S(1)}, f32[128,2048]{1,0:T(8,128)}, u32[]{:S(2)}) copy-start(f32[128,2048]{1,0:T(8,128)} %get-tuple-element.224) | copy-start | bytes 3145732
  (50 other events, 133.1 us)
Sparse Core Ops, SparseCore 0:
  9.9 155.4 all-gather.20
  247.1 35.8 all-gather.16
  284.9 87.6 all-gather.18
  374.8 35.3 all-gather.22
  411.8 87.5 all-gather.24
  501.2 297.2 all-gather.26
  800.3 297.2 all-gather.28
  1185.6 35.1 reduce-scatter.24
  1224.6 35.1 reduce-scatter.26
  1263.3 86.3 reduce-scatter.14
  1353.1 86.3 reduce-scatter.20
  1443.1 86.3 reduce-scatter.16
  1532.9 86.4 reduce-scatter.18
  1622.2 288.6 reduce-scatter.22
  1914.1 288.6 reduce-scatter.28
  2204.5 87.5 all-gather.30
  2295.2 494.7 all-reduce.14
